TPU v7x, 512 devices: a whole 4x8x8 slice. The times are simulated.
512 devices in a mesh: cam: 8 (over y_lo, x), sp: 64 (over z, y_hi, core).
Axes of the slice: x: 4, y: 8 (y_hi: 4, y_lo: 2; y = y_hi * 2 + y_lo), z: 8, core: 2. Of those that a mesh axis runs over, the one named last changes fastest.
Arguments:
- q_self: bfloat16 [8, 2048, 2048], P('cam', 'sp'), may hold values from -8 to 8
- keys: bfloat16 [8, 2048, 2048], P('cam', 'sp'), may hold values from -4 to 4
- values: bfloat16 [8, 2048, 2048], P('cam', 'sp'), may hold values from -4 to 4
- q_cross: bfloat16 [8, 2048, 2048], P('cam', 'sp'), may hold values from -8 to 8
- timestep: int32 [1], replicated, may hold values from 0 to 49
- mod_table: float32 [50, 2, 2048], replicated, may hold values from 0.5 to 3
Outputs:
- block_out: bfloat16 [8, 2048, 2048], P('cam', 'sp')
All inputs are finite; a program needn't handle non-finite values.
Results may differ from a plain program's by a relative error of at most 0.0042.
Values may be sent and summed in bfloat16 or wider, within the bound.
No kernel may reach another device: no remote copies, remote signals or barrier semaphores. Data moves between devices by JAX's collectives and lax.ppermute only.
A program may use at most 64 MiB of HBM per device.

v0:
```python
import math
import jax
import jax.numpy as jnp
from jax import lax
from jax.sharding import PartitionSpec as P

HEADS = 16


def passed_along(value, axis, steps):
    count = lax.axis_size(axis)
    pairs = [(source, (source + steps) % count) for source in range(count)]
    return lax.ppermute(value, axis, pairs)


def pick_block(extent, ceiling):
    block_size = min(ceiling, extent)
    while extent % block_size:
        block_size = block_size - 1
    return block_size


def attend(queries, key_rows, value_rows, score_scale):
    query_count, head_dim = queries.shape
    key_count = key_rows.shape[0]
    query_block = pick_block(query_count, 512)
    key_block = pick_block(key_count, 1024)
    key_blocks = key_rows.reshape(key_count // key_block, key_block, head_dim)
    value_blocks = value_rows.reshape(key_count // key_block, key_block, head_dim)

    def per_query(query_part):

        def absorb(state_now, pair_now):
            numerator, runmax, totals = state_now
            key_part, value_part = pair_now
            scores = (
                jnp.einsum("qd,kd->qk", query_part, key_part, preferred_element_type=jnp.float32)
                * score_scale
            )
            newmax = jnp.maximum(runmax, jnp.max(scores, axis=1))
            factor = jnp.exp(runmax - newmax)
            weights = jnp.exp(scores - newmax[:, None])
            totals = totals * factor + jnp.sum(weights, axis=1)
            numerator = numerator * factor[:, None] + jnp.dot(
                weights.astype(jnp.bfloat16), value_part, preferred_element_type=jnp.float32
            )
            return ((numerator, newmax, totals), None)

        start_state = (
            jnp.zeros((query_block, head_dim), jnp.float32),
            jnp.full((query_block,), -jnp.inf, jnp.float32),
            jnp.zeros((query_block,), jnp.float32),
        )
        final_state, _ = lax.scan(absorb, start_state, (key_blocks, value_blocks))
        return final_state

    numerator, runmax, totals = lax.map(
        per_query, queries.reshape(query_count // query_block, query_block, head_dim)
    )
    return (
        numerator.reshape(query_count, head_dim),
        runmax.reshape(query_count),
        totals.reshape(query_count),
    )


def local(q_self, keys, values, q_cross, timestep, mod_table):
    row_count = q_self.shape[1]
    full_width = q_self.shape[2]
    head_count = HEADS
    head_dim = full_width // head_count
    groups = lax.axis_size("sp")
    copies = groups // head_count
    part_rows = row_count // copies
    score_scale = 1.0 / math.sqrt(head_dim)
    query_heads = q_self[0].reshape(row_count, head_count, head_dim)
    key_heads = keys[0].reshape(row_count, head_count, head_dim)
    value_heads = values[0].reshape(row_count, head_count, head_dim)

    def quartered(tensor):
        return (
            tensor.reshape(copies, part_rows, head_count, head_dim)
            .transpose(2, 0, 1, 3)
            .reshape(groups, part_rows, head_dim)
        )

    spread = jnp.broadcast_to(
        query_heads.transpose(1, 0, 2)[:, None], (head_count, copies, row_count, head_dim)
    )
    queries_here = lax.all_to_all(
        spread.reshape(groups, row_count, head_dim), "sp", split_axis=0, concat_axis=1, tiled=True
    )
    keys_here = lax.all_to_all(quartered(key_heads), "sp", split_axis=0, concat_axis=1, tiled=True)
    values_here = lax.all_to_all(
        quartered(value_heads), "sp", split_axis=0, concat_axis=1, tiled=True
    )
    numerator, runmax, totals = attend(queries_here[0], keys_here[0], values_here[0], score_scale)
    numerator, runmax, totals = (
        lax.all_to_all(
            numerator.reshape(groups, row_count, head_dim),
            "sp",
            split_axis=0,
            concat_axis=0,
            tiled=True,
        ),
        lax.all_to_all(
            runmax.reshape(groups, row_count), "sp", split_axis=0, concat_axis=0, tiled=True
        ),
        lax.all_to_all(
            totals.reshape(groups, row_count), "sp", split_axis=0, concat_axis=0, tiled=True
        ),
    )
    numerator = numerator.reshape(head_count, copies, row_count, head_dim)
    runmax = runmax.reshape(head_count, copies, row_count)
    totals = totals.reshape(head_count, copies, row_count)
    topmax = jnp.max(runmax, axis=1)
    factor = jnp.exp(runmax - topmax[:, None])
    numerator = jnp.sum(numerator * factor[..., None], axis=1)
    totals = jnp.sum(totals * factor, axis=1)
    self_out = (
        (numerator / totals[..., None])
        .astype(jnp.bfloat16)
        .transpose(1, 0, 2)
        .reshape(row_count, full_width)
    )
    left_keys, left_values = passed_along((keys[0], values[0]), "cam", 1)
    right_keys, right_values = passed_along((keys[0], values[0]), "cam", -1)
    near_keys = jnp.concatenate([left_keys, right_keys], axis=0).reshape(
        2 * row_count, head_count, head_dim
    )
    near_values = jnp.concatenate([left_values, right_values], axis=0).reshape(
        2 * row_count, head_count, head_dim
    )
    cross_queries = q_cross[0].reshape(row_count, head_count, head_dim)
    scores = (
        jnp.einsum("qhd,khd->hqk", cross_queries, near_keys, preferred_element_type=jnp.float32)
        * score_scale
    )
    row_peak = jnp.max(scores, axis=2)
    weights = jnp.exp(scores - row_peak[..., None])
    totals = jnp.sum(weights, axis=2)
    numerator = jnp.einsum(
        "hqk,khd->qhd",
        weights.astype(jnp.bfloat16),
        near_values,
        preferred_element_type=jnp.float32,
    )
    cross_out = (numerator / totals.T[:, :, None]).reshape(row_count, full_width)
    selector = (jnp.arange(mod_table.shape[0]) == timestep[0]).astype(jnp.float32)
    gate_rows = jnp.tensordot(selector, mod_table, axes=1, precision=lax.Precision.HIGHEST)
    mixed = gate_rows[0] * self_out.astype(jnp.float32) + gate_rows[1] * cross_out
    return mixed.astype(jnp.bfloat16)[None]


def solution(mesh):
    placed = (
        P("cam", "sp", None),
        P("cam", "sp", None),
        P("cam", "sp", None),
        P("cam", "sp", None),
        P(),
        P(),
    )
    return jax.shard_map(
        local, mesh=mesh, in_specs=placed, out_specs=P("cam", "sp", None), check_vma=False
    )
```

profile of v0, /device:TPU:1, one launch (start us, length us, event | category | flops | bytes accessed | tf_op | source)
XLA Modules:
  0.0 154.9 jit_solution(5644704901470905810)
XLA Ops:
  0.0 1.7 %copy.28 = bf16[16,4,8,128]{3,2,1,0:T(8,128)(2,1)} copy(bf16[16,4,8,128]{3,2,0,1:T(8,128)(2,1)} %bitcast.112) | data formatting | bytes 262144 | tf_op jit(solution)/shard_map/transpose | solution.py:83
  1.7 17.8 %all-to-all-start.1 = ((bf16[64,8,128]{2,1,0:T(8,128)(2,1)}), bf16[64,8,128]{2,1,0:T(8,128)(2,1)S(1)}, u32[]{:S(2)}, u32[]{:S(2)}) async-start(bf16[64,8,128]{2,1,0:T(8,128)(2,1)} %bitcast.15), calls=%async_computation.1 | async-start | bytes 262144 | tf_op jit(solution)/shard_map/all_to_all | solution.py:93
  20.1 12.4 %all-to-all-done.1 = bf16[64,8,128]{2,1,0:T(8,128)(2,1)S(1)} async-done(((bf16[64,8,128]{2,1,0:T(8,128)(2,1)}), bf16[64,8,128]{2,1,0:T(8,128)(2,1)S(1)}, u32[]{:S(2)}, u32[]{:S(2)}) %all-to-all-start.1) | async-done | bytes 131104 | tf_op jit(solution)/shard_map/all_to_all | solution.py:93
  32.5 4.6 %all-to-all-start.2 = ((bf16[64,8,128]{2,1,0:T(8,128)(2,1)}), bf16[64,8,128]{2,1,0:T(8,128)(2,1)S(1)}, u32[]{:S(2)}, u32[]{:S(2)}) async-start(bf16[64,8,128]{2,1,0:T(8,128)(2,1)} %bitcast.19), calls=%async_computation.2 | async-start | bytes 262144 | tf_op jit(solution)/shard_map/all_to_all | solution.py:94
  37.2 13.4 %all-to-all-done.2 = bf16[64,8,128]{2,1,0:T(8,128)(2,1)S(1)} async-done(((bf16[64,8,128]{2,1,0:T(8,128)(2,1)}), bf16[64,8,128]{2,1,0:T(8,128)(2,1)S(1)}, u32[]{:S(2)}, u32[]{:S(2)}) %all-to-all-start.2) | async-done | bytes 131104 | tf_op jit(solution)/shard_map/all_to_all | solution.py:94
  50.6 0.9 broadcast_in_dim.18
  51.5 4.5 %all-to-all-start = ((bf16[64,32,128]{2,1,0:T(8,128)(2,1)}), bf16[64,32,128]{2,1,0:T(8,128)(2,1)S(1)}, u32[]{:S(2)}, u32[]{:S(2)}) async-start(bf16[64,32,128]{2,1,0:T(8,128)(2,1)} %bitcast.11), calls=%async_computation | async-start | bytes 1048576 | tf_op jit(solution)/shard_map/all_to_all | solution.py:90
  56.0 19.6 %all-to-all-done = bf16[64,32,128]{2,1,0:T(8,128)(2,1)S(1)} async-done(((bf16[64,32,128]{2,1,0:T(8,128)(2,1)}), bf16[64,32,128]{2,1,0:T(8,128)(2,1)S(1)}, u32[]{:S(2)}, u32[]{:S(2)}) %all-to-all-start) | async-done | bytes 524320 | tf_op jit(solution)/shard_map/all_to_all | solution.py:90
  75.6 6.8 %while.14 = (s32[]{:T(128)}, f32[4,512,128]{2,1,0:T(8,128)}, f32[4,512]{1,0:T(4,128)S(1)}, f32[4,512]{1,0:T(4,128)S(1)}, bf16[4,512,128]{2,1,0:T(8,128)(2,1)S(1)...) while((s32[]{:T(128)}, f32[4,512,128]{2,1,0:T(8,128)}, ...), condition=%wide.region_3.0_spmd, body=%wide.region_0.3_spmd.sunk | while | flops 135857664 | bytes 3830377 | solution.py:57
  76.2 1.0 fusion.43
  77.9 1.0 fusion.43
  79.6 1.0 fusion.43
  81.3 1.0 fusion.43
  83.0 5.9 %all-to-all-start.4 = ((f32[64,1,32]{2,1,0:T(1,128)}), f32[64,1,32]{2,1,0:T(1,128)S(1)}, u32[]{:S(2)}, u32[]{:S(2)}) async-start(f32[64,1,32]{2,1,0:T(1,128)} %bitcast.23), calls=%async_computation.4 | async-start | bytes 65536 | tf_op jit(solution)/shard_map/all_to_all | solution.py:106
  89.0 11.6 %all-to-all-done.4 = f32[64,1,32]{2,1,0:T(1,128)S(1)} async-done(((f32[64,1,32]{2,1,0:T(1,128)}), f32[64,1,32]{2,1,0:T(1,128)S(1)}, u32[]{:S(2)}, u32[]{:S(2)}) %all-to-all-start.4) | async-done | bytes 8224 | tf_op jit(solution)/shard_map/all_to_all | solution.py:106
  100.6 15.8 %all_to_all.56 = f32[64,1,32]{2,1,0:T(1,128)S(1)} all-to-all(f32[64,1,32]{2,1,0:T(1,128)S(1)} %bitcast.109), channel_id=1, replica_groups=mesh['cam'=8,'sp'=64] {'sp'}, dimensions={0} | all-to-all | bytes 16384 | tf_op jit(solution)/shard_map/all_to_all | solution.py:109
  116.4 4.9 %all-to-all-start.3 = ((f32[64,32,128]{2,1,0:T(8,128)}), f32[64,32,128]{2,1,0:T(8,128)S(1)}, u32[]{:S(2)}, u32[]{:S(2)}) async-start(f32[64,32,128]{2,1,0:T(8,128)} %bitcast.106), calls=%async_computation.3 | async-start | bytes 2097152 | tf_op jit(solution)/shard_map/all_to_all | solution.py:99
  121.3 3.1 %collective-permute-start.2 = (bf16[32,2048]{1,0:T(8,128)(2,1)S(1)}, bf16[32,2048]{1,0:T(8,128)(2,1)S(1)}, u32[]{:S(2)}, u32[]{:S(2)}) collective-permute-start(bf16[32,2048]{1,0:T(8,128)(2,1)S(1)} %bitcast.113), channel_id=1, source_target_pairs={{0,64},{64,128},{128,192},{192,256},{256,320},{320,384},{384,448},... | collective-permute-start | bytes 393224 | tf_op jit(solution)/shard_map/ppermute | solution.py:13
  124.4 4.3 %collective-permute-start.3 = (bf16[32,2048]{1,0:T(8,128)(2,1)S(1)}, bf16[32,2048]{1,0:T(8,128)(2,1)S(1)}, u32[]{:S(2)}, u32[]{:S(2)}) collective-permute-start(bf16[32,2048]{1,0:T(8,128)(2,1)S(1)} %bitcast.114), channel_id=1, source_target_pairs={{0,448},{64,0},{128,64},{192,128},{256,192},{320,256},{384,320},{4... | collective-permute-start | bytes 393224 | tf_op jit(solution)/shard_map/ppermute | solution.py:13
  128.7 1.9 %collective-permute-start = (bf16[32,2048]{1,0:T(8,128)(2,1)S(1)}, bf16[32,2048]{1,0:T(8,128)(2,1)S(1)}, u32[]{:S(2)}, u32[]{:S(2)}) collective-permute-start(bf16[32,2048]{1,0:T(8,128)(2,1)S(1)} %bitcast.116), channel_id=1, source_target_pairs={{0,64},{64,128},{128,192},{192,256},{256,320},{320,384},{384,448},... | collective-permute-start | bytes 393224 | tf_op jit(solution)/shard_map/ppermute | solution.py:13
  130.7 5.5 %collective-permute-start.1 = (bf16[32,2048]{1,0:T(8,128)(2,1)S(1)}, bf16[32,2048]{1,0:T(8,128)(2,1)S(1)}, u32[]{:S(2)}, u32[]{:S(2)}) collective-permute-start(bf16[32,2048]{1,0:T(8,128)(2,1)S(1)} %bitcast.117), channel_id=1, source_target_pairs={{0,448},{64,0},{128,64},{192,128},{256,192},{320,256},{384,320},{4... | collective-permute-start | bytes 393224 | tf_op jit(solution)/shard_map/ppermute | solution.py:13
  136.8 0.9 fusion.13
  137.8 12.3 %collective-permute-done.2 = bf16[32,2048]{1,0:T(8,128)(2,1)S(1)} collective-permute-done((bf16[32,2048]{1,0:T(8,128)(2,1)S(1)}, bf16[32,2048]{1,0:T(8,128)(2,1)S(1)}, u32[]{:S(2)}, u32[]{:S(2)}) %collective-permute-start.2) | collective-permute-done | bytes 131104 | tf_op jit(solution)/shard_map/ppermute | solution.py:13
  150.7 2.2 %collective-permute-done = bf16[32,2048]{1,0:T(8,128)(2,1)S(1)} collective-permute-done((bf16[32,2048]{1,0:T(8,128)(2,1)S(1)}, bf16[32,2048]{1,0:T(8,128)(2,1)S(1)}, u32[]{:S(2)}, u32[]{:S(2)}) %collective-permute-start) | collective-permute-done | bytes 131104 | tf_op jit(solution)/shard_map/ppermute | solution.py:13
  (59 shorter events, 6.5 us)
Async XLA Ops:
  0.0 136.8 %copy-start = (f32[50,2,2048]{2,1,0:T(2,128)S(1)}, f32[50,2,2048]{2,1,0:T(2,128)}, u32[]{:S(2)}) copy-start(f32[50,2,2048]{2,1,0:T(2,128)} %param.13) | copy-start | bytes 2457604
  1.7 17.8 %copy-start.4 = (bf16[1,32,2048]{2,1,0:T(8,128)(2,1)S(1)}, bf16[1,32,2048]{2,1,0:T(8,128)(2,1)}, u32[]{:S(2)}) copy-start(bf16[1,32,2048]{2,1,0:T(8,128)(2,1)} %param.10) | copy-start | bytes 393220
  1.7 30.9 %all-to-all-start.1 = ((bf16[64,8,128]{2,1,0:T(8,128)(2,1)}), bf16[64,8,128]{2,1,0:T(8,128)(2,1)S(1)}, u32[]{:S(2)}, u32[]{:S(2)}) async-start(bf16[64,8,128]{2,1,0:T(8,128)(2,1)} %bitcast.15), calls=%async_computation.1 | async-start | bytes 262144 | tf_op jit(solution)/shard_map/all_to_all | solution.py:93
  32.5 4.6 %copy-start.1 = (bf16[1,32,2048]{2,1,0:T(8,128)(2,1)S(1)}, bf16[1,32,2048]{2,1,0:T(8,128)(2,1)}, u32[]{:S(2)}) copy-start(bf16[1,32,2048]{2,1,0:T(8,128)(2,1)} %param.8) | copy-start | bytes 393220
  32.5 18.0 %all-to-all-start.2 = ((bf16[64,8,128]{2,1,0:T(8,128)(2,1)}), bf16[64,8,128]{2,1,0:T(8,128)(2,1)S(1)}, u32[]{:S(2)}, u32[]{:S(2)}) async-start(bf16[64,8,128]{2,1,0:T(8,128)(2,1)} %bitcast.19), calls=%async_computation.2 | async-start | bytes 262144 | tf_op jit(solution)/shard_map/all_to_all | solution.py:94
  51.5 24.1 %all-to-all-start = ((bf16[64,32,128]{2,1,0:T(8,128)(2,1)}), bf16[64,32,128]{2,1,0:T(8,128)(2,1)S(1)}, u32[]{:S(2)}, u32[]{:S(2)}) async-start(bf16[64,32,128]{2,1,0:T(8,128)(2,1)} %bitcast.11), calls=%async_computation | async-start | bytes 1048576 | tf_op jit(solution)/shard_map/all_to_all | solution.py:90
  83.0 17.6 %all-to-all-start.4 = ((f32[64,1,32]{2,1,0:T(1,128)}), f32[64,1,32]{2,1,0:T(1,128)S(1)}, u32[]{:S(2)}, u32[]{:S(2)}) async-start(f32[64,1,32]{2,1,0:T(1,128)} %bitcast.23), calls=%async_computation.4 | async-start | bytes 65536 | tf_op jit(solution)/shard_map/all_to_all | solution.py:106
  116.4 4.9 %copy-start.3 = (bf16[1,32,2048]{2,1,0:T(8,128)(2,1)S(1)}, bf16[1,32,2048]{2,1,0:T(8,128)(2,1)}, u32[]{:S(2)}) copy-start(bf16[1,32,2048]{2,1,0:T(8,128)(2,1)} %param.9) | copy-start | bytes 393220
  116.4 37.0 %all-to-all-start.3 = ((f32[64,32,128]{2,1,0:T(8,128)}), f32[64,32,128]{2,1,0:T(8,128)S(1)}, u32[]{:S(2)}, u32[]{:S(2)}) async-start(f32[64,32,128]{2,1,0:T(8,128)} %bitcast.106), calls=%async_computation.3 | async-start | bytes 2097152 | tf_op jit(solution)/shard_map/all_to_all | solution.py:99
  121.3 28.8 %collective-permute-start.2 = (bf16[32,2048]{1,0:T(8,128)(2,1)S(1)}, bf16[32,2048]{1,0:T(8,128)(2,1)S(1)}, u32[]{:S(2)}, u32[]{:S(2)}) collective-permute-start(bf16[32,2048]{1,0:T(8,128)(2,1)S(1)} %bitcast.113), channel_id=1, source_target_pairs={{0,64},{64,128},{128,192},{192,256},{256,320},{320,384},{384,448},... | collective-permute-start | bytes 393224 | tf_op jit(solution)/shard_map/ppermute | solution.py:13
  124.4 25.6 %collective-permute-start.3 = (bf16[32,2048]{1,0:T(8,128)(2,1)S(1)}, bf16[32,2048]{1,0:T(8,128)(2,1)S(1)}, u32[]{:S(2)}, u32[]{:S(2)}) collective-permute-start(bf16[32,2048]{1,0:T(8,128)(2,1)S(1)} %bitcast.114), channel_id=1, source_target_pairs={{0,448},{64,0},{128,64},{192,128},{256,192},{320,256},{384,320},{4... | collective-permute-start | bytes 393224 | tf_op jit(solution)/shard_map/ppermute | solution.py:13
  128.7 24.2 %collective-permute-start = (bf16[32,2048]{1,0:T(8,128)(2,1)S(1)}, bf16[32,2048]{1,0:T(8,128)(2,1)S(1)}, u32[]{:S(2)}, u32[]{:S(2)}) collective-permute-start(bf16[32,2048]{1,0:T(8,128)(2,1)S(1)} %bitcast.116), channel_id=1, source_target_pairs={{0,64},{64,128},{128,192},{192,256},{256,320},{320,384},{384,448},... | collective-permute-start | bytes 393224 | tf_op jit(solution)/shard_map/ppermute | solution.py:13
  130.7 22.2 %collective-permute-start.1 = (bf16[32,2048]{1,0:T(8,128)(2,1)S(1)}, bf16[32,2048]{1,0:T(8,128)(2,1)S(1)}, u32[]{:S(2)}, u32[]{:S(2)}) collective-permute-start(bf16[32,2048]{1,0:T(8,128)(2,1)S(1)} %bitcast.117), channel_id=1, source_target_pairs={{0,448},{64,0},{128,64},{192,128},{256,192},{320,256},{384,320},{4... | collective-permute-start | bytes 393224 | tf_op jit(solution)/shard_map/ppermute | solution.py:13
  136.8 0.9 copy-start.2
where the time goes:
time: 156 us; the launch traced here: 155 us
  waiting for transfers between devices  71.6 us (46%)
  starting transfers between devices  52.3 us (34%)
  blocking collectives  15.8 us (10%)
  matrix products  6.9 us (4%)
  local copies, waits for them, and re-layouts  4.86 us (3%)
  other arithmetic  2.36 us (2%)
    all_to_all x1, waiting for transfers between devices, local(): lax.all_to_all(spread.reshape(groups, row_count, head_dim), 'sp', split_a...  19.6 us
    all_to_all x1, starting transfers between devices, local(): lax.all_to_all(quartered(key_heads), 'sp', split_axis=0, concat_axis=1, t...  17.8 us
    all_to_all x1, blocking collectives, local(): lax.all_to_all(totals.reshape(groups, row_count), 'sp', split_axis=0, con...  15.8 us
    ppermute x4, starting transfers between devices, passed_along(): return lax.ppermute(value, axis, pairs)  14.8 us
    ppermute x4, waiting for transfers between devices, passed_along(): return lax.ppermute(value, axis, pairs)  14.5 us
    all_to_all x1, waiting for transfers between devices, local(): lax.all_to_all(quartered(value_heads), 'sp', split_axis=0, concat_axis=1,...  13.4 us
    all_to_all x1, waiting for transfers between devices, local(): lax.all_to_all(quartered(key_heads), 'sp', split_axis=0, concat_axis=1, t...  12.4 us
    all_to_all x1, waiting for transfers between devices, local(): lax.all_to_all(runmax.reshape(groups, row_count), 'sp', split_axis=0, con...  11.6 us
  transfers between devices with their start and end apart: 9, of which 6 were waited for; matrix products, arithmetic and copies ran while one was open for 2% of the time, Pallas kernels for 0%

commit v1 on v0

--- a/solution.py
+++ b/solution.py
@@ -87,8 +87,16 @@
     spread = jnp.broadcast_to(
         query_heads.transpose(1, 0, 2)[:, None], (head_count, copies, row_count, head_dim)
     )
-    queries_here = lax.all_to_all(
-        spread.reshape(groups, row_count, head_dim), "sp", split_axis=0, concat_axis=1, tiled=True
+    queries_here = jnp.concatenate(
+        lax.all_to_all(
+            jnp.stack(
+                jnp.split(spread.reshape(groups, row_count, head_dim), lax.axis_size("sp"), axis=0)
+            ),
+            "sp",
+            0,
+            0,
+        ),
+        axis=1,
     )
     keys_here = lax.all_to_all(quartered(key_heads), "sp", split_axis=0, concat_axis=1, tiled=True)
     values_here = lax.all_to_all(

time: 156 us -> 188 us (1.21)
  local copies, waits for them, and re-layouts: 4.86 us -> 42.1 us
  waiting for transfers between devices: 71.6 us -> 57.7 us
  starting transfers between devices: 52.3 us -> 60.7 us
    unnamed x12 -> x75, local copies, waits for them, and re-layouts: 0.06 us -> 37.5 us
    all_to_all x1, waiting for transfers between devices: 12.4 us -> 0.01 us  [local(): lax.all_to_all(quartered(key_heads), 'sp', split_axis=0, concat_axis=1, t...]
    all_to_all x1, starting transfers between devices: 4.57 us -> 12.7 us  [local(): lax.all_to_all(quartered(value_heads), 'sp', split_axis=0, concat_axis=1,...]
  transfers between devices with their start and end apart: 9 -> 9, of which waited for: 6 -> 5; matrix products, arithmetic and copies ran while one was open for 2% -> 22% of each run, Pallas kernels for 0% -> 0%
where the time goes in v1:
time: 188 us; the launch traced here: 187 us
  starting transfers between devices  60.7 us (32%)
  waiting for transfers between devices  57.7 us (31%)
  local copies, waits for them, and re-layouts  42.1 us (22%)
  blocking collectives  15.8 us (8%)
  matrix products  6.89 us (4%)
  other arithmetic  2.36 us (1%)
    unnamed x75, local copies, waits for them, and re-layouts  37.5 us
    all_to_all x1, waiting for transfers between devices, local(): lax.all_to_all(jnp.stack(jnp.split(spread.reshape(groups, row_count, head...  19.3 us
    all_to_all x1, starting transfers between devices, local(): lax.all_to_all(quartered(key_heads), 'sp', split_axis=0, concat_axis=1, t...  17.8 us
    all_to_all x1, blocking collectives, local(): lax.all_to_all(totals.reshape(groups, row_count), 'sp', split_axis=0, con...  15.8 us
    ppermute x4, waiting for transfers between devices, passed_along(): return lax.ppermute(value, axis, pairs)  14.8 us
    ppermute x4, starting transfers between devices, passed_along(): return lax.ppermute(value, axis, pairs)  14.8 us
    all_to_all x1, starting transfers between devices, local(): lax.all_to_all(quartered(value_heads), 'sp', split_axis=0, concat_axis=1,...  12.7 us
    all_to_all x1, waiting for transfers between devices, local(): lax.all_to_all(quartered(value_heads), 'sp', split_axis=0, concat_axis=1,...  11.9 us
  transfers between devices with their start and end apart: 9, of which 5 were waited for; matrix products, arithmetic and copies ran while one was open for 22% of the time, Pallas kernels for 0%

profile of v1, /device:TPU:1, one launch (start us, length us, event | category | flops | bytes accessed | tf_op | source)
XLA Modules:
  0.0 186.7 jit_solution(7588343600462875545)
XLA Ops:
  0.0 1.7 copy.154
  1.7 17.8 %all-to-all-start.1 = ((bf16[64,8,128]{2,1,0:T(8,128)(2,1)}), bf16[64,8,128]{2,1,0:T(8,128)(2,1)S(1)}, u32[]{:S(2)}, u32[]{:S(2)}) async-start(bf16[64,8,128]{2,1,0:T(8,128)(2,1)} %bitcast.79), calls=%async_computation.1 | async-start | bytes 262144 | tf_op jit(solution)/shard_map/all_to_all | solution.py:101
  57.2 12.7 %all-to-all-start.2 = ((bf16[64,8,128]{2,1,0:T(8,128)(2,1)}), bf16[64,8,128]{2,1,0:T(8,128)(2,1)S(1)}, u32[]{:S(2)}, u32[]{:S(2)}) async-start(bf16[64,8,128]{2,1,0:T(8,128)(2,1)} %bitcast.83), calls=%async_computation.2 | async-start | bytes 262144 | tf_op jit(solution)/shard_map/all_to_all | solution.py:102
  71.1 11.9 %all-to-all-done.2 = bf16[64,8,128]{2,1,0:T(8,128)(2,1)S(1)} async-done(((bf16[64,8,128]{2,1,0:T(8,128)(2,1)}), bf16[64,8,128]{2,1,0:T(8,128)(2,1)S(1)}, u32[]{:S(2)}, u32[]{:S(2)}) %all-to-all-start.2) | async-done | bytes 131104 | tf_op jit(solution)/shard_map/all_to_all | solution.py:102
  83.0 4.5 %all-to-all-start = ((bf16[64,1,32,128]{3,2,1,0:T(8,128)(2,1)}), bf16[64,1,32,128]{3,2,1,0:T(8,128)(2,1)S(1)}, u32[]{:S(2)}, u32[]{:S(2)}) async-start(bf16[64,1,32,128]{3,2,1,0:T(8,128)(2,1)} %constant_dynamic-update-slice_fusion), calls=%async_computation | async-start | bytes 1048576 | tf_op jit(solution)/shard_map/all_to_all | solution.py:91
  87.5 19.3 %all-to-all-done = bf16[64,1,32,128]{3,2,1,0:T(8,128)(2,1)S(1)} async-done(((bf16[64,1,32,128]{3,2,1,0:T(8,128)(2,1)}), bf16[64,1,32,128]{3,2,1,0:T(8,128)(2,1)S(1)}, u32[]{:S(2)}, u32[]{:S(2)}) %all-to-all-start) | async-done | bytes 524320 | tf_op jit(solution)/shard_map/all_to_all | solution.py:91
  106.9 6.8 %while.14 = (s32[]{:T(128)}, f32[4,512,128]{2,1,0:T(8,128)}, f32[4,512]{1,0:T(4,128)S(1)}, f32[4,512]{1,0:T(4,128)S(1)}, bf16[4,512,128]{2,1,0:T(8,128)(2,1)S(1)...) while((s32[]{:T(128)}, f32[4,512,128]{2,1,0:T(8,128)}, ...), condition=%wide.region_3.0_spmd, body=%wide.region_0.3_spmd.sunk | while | flops 135857664 | bytes 3830377 | solution.py:57
  107.5 1.0 fusion.43
  109.2 1.0 fusion.43
  110.9 1.0 fusion.43
  112.6 1.0 fusion.43
  113.6 0.7 all_to_all.42
  114.3 6.1 %all-to-all-start.4 = ((f32[64,1,32]{2,1,0:T(1,128)}), f32[64,1,32]{2,1,0:T(1,128)S(1)}, u32[]{:S(2)}, u32[]{:S(2)}) async-start(f32[64,1,32]{2,1,0:T(1,128)} %bitcast.87), calls=%async_computation.4 | async-start | bytes 65536 | tf_op jit(solution)/shard_map/all_to_all | solution.py:114
  120.5 11.7 %all-to-all-done.4 = f32[64,1,32]{2,1,0:T(1,128)S(1)} async-done(((f32[64,1,32]{2,1,0:T(1,128)}), f32[64,1,32]{2,1,0:T(1,128)S(1)}, u32[]{:S(2)}, u32[]{:S(2)}) %all-to-all-start.4) | async-done | bytes 8224 | tf_op jit(solution)/shard_map/all_to_all | solution.py:114
  132.2 15.8 %all_to_all.52 = f32[64,1,32]{2,1,0:T(1,128)S(1)} all-to-all(f32[64,1,32]{2,1,0:T(1,128)S(1)} %bitcast.429), channel_id=1, replica_groups=mesh['cam'=8,'sp'=64] {'sp'}, dimensions={0} | all-to-all | bytes 16384 | tf_op jit(solution)/shard_map/all_to_all | solution.py:117
  148.0 4.9 %all-to-all-start.3 = ((f32[64,32,128]{2,1,0:T(8,128)}), f32[64,32,128]{2,1,0:T(8,128)S(1)}, u32[]{:S(2)}, u32[]{:S(2)}) async-start(f32[64,32,128]{2,1,0:T(8,128)} %bitcast.426), calls=%async_computation.3 | async-start | bytes 2097152 | tf_op jit(solution)/shard_map/all_to_all | solution.py:107
  152.9 3.1 %collective-permute-start.2 = (bf16[32,2048]{1,0:T(8,128)(2,1)S(1)}, bf16[32,2048]{1,0:T(8,128)(2,1)S(1)}, u32[]{:S(2)}, u32[]{:S(2)}) collective-permute-start(bf16[32,2048]{1,0:T(8,128)(2,1)S(1)} %bitcast.433), channel_id=1, source_target_pairs={{0,64},{64,128},{128,192},{192,256},{256,320},{320,384},{384,448},... | collective-permute-start | bytes 393224 | tf_op jit(solution)/shard_map/ppermute | solution.py:13
  156.0 4.3 %collective-permute-start.3 = (bf16[32,2048]{1,0:T(8,128)(2,1)S(1)}, bf16[32,2048]{1,0:T(8,128)(2,1)S(1)}, u32[]{:S(2)}, u32[]{:S(2)}) collective-permute-start(bf16[32,2048]{1,0:T(8,128)(2,1)S(1)} %bitcast.434), channel_id=1, source_target_pairs={{0,448},{64,0},{128,64},{192,128},{256,192},{320,256},{384,320},{4... | collective-permute-start | bytes 393224 | tf_op jit(solution)/shard_map/ppermute | solution.py:13
  160.3 1.9 %collective-permute-start = (bf16[32,2048]{1,0:T(8,128)(2,1)S(1)}, bf16[32,2048]{1,0:T(8,128)(2,1)S(1)}, u32[]{:S(2)}, u32[]{:S(2)}) collective-permute-start(bf16[32,2048]{1,0:T(8,128)(2,1)S(1)} %bitcast.436), channel_id=1, source_target_pairs={{0,64},{64,128},{128,192},{192,256},{256,320},{320,384},{384,448},... | collective-permute-start | bytes 393224 | tf_op jit(solution)/shard_map/ppermute | solution.py:13
  162.2 5.5 %collective-permute-start.1 = (bf16[32,2048]{1,0:T(8,128)(2,1)S(1)}, bf16[32,2048]{1,0:T(8,128)(2,1)S(1)}, u32[]{:S(2)}, u32[]{:S(2)}) collective-permute-start(bf16[32,2048]{1,0:T(8,128)(2,1)S(1)} %bitcast.437), channel_id=1, source_target_pairs={{0,448},{64,0},{128,64},{192,128},{256,192},{320,256},{384,320},{4... | collective-permute-start | bytes 393224 | tf_op jit(solution)/shard_map/ppermute | solution.py:13
  168.4 0.9 fusion.13
  169.3 12.6 %collective-permute-done.2 = bf16[32,2048]{1,0:T(8,128)(2,1)S(1)} collective-permute-done((bf16[32,2048]{1,0:T(8,128)(2,1)S(1)}, bf16[32,2048]{1,0:T(8,128)(2,1)S(1)}, u32[]{:S(2)}, u32[]{:S(2)}) %collective-permute-start.2) | collective-permute-done | bytes 131104 | tf_op jit(solution)/shard_map/ppermute | solution.py:13
  182.5 2.2 %collective-permute-done = bf16[32,2048]{1,0:T(8,128)(2,1)S(1)} collective-permute-done((bf16[32,2048]{1,0:T(8,128)(2,1)S(1)}, bf16[32,2048]{1,0:T(8,128)(2,1)S(1)}, u32[]{:S(2)}, u32[]{:S(2)}) %collective-permute-start) | collective-permute-done | bytes 131104 | tf_op jit(solution)/shard_map/ppermute | solution.py:13
  186.0 0.7 add_convert_fusion
  (123 shorter events, 43.3 us)
Async XLA Ops:
  0.0 168.4 %copy-start = (f32[50,2,2048]{2,1,0:T(2,128)S(1)}, f32[50,2,2048]{2,1,0:T(2,128)}, u32[]{:S(2)}) copy-start(f32[50,2,2048]{2,1,0:T(2,128)} %param.13) | copy-start | bytes 2457604
  1.7 17.8 %copy-start.1 = (bf16[1,32,2048]{2,1,0:T(8,128)(2,1)S(1)}, bf16[1,32,2048]{2,1,0:T(8,128)(2,1)}, u32[]{:S(2)}) copy-start(bf16[1,32,2048]{2,1,0:T(8,128)(2,1)} %param.8) | copy-start | bytes 393220
  1.7 55.5 %all-to-all-start.1 = ((bf16[64,8,128]{2,1,0:T(8,128)(2,1)}), bf16[64,8,128]{2,1,0:T(8,128)(2,1)S(1)}, u32[]{:S(2)}, u32[]{:S(2)}) async-start(bf16[64,8,128]{2,1,0:T(8,128)(2,1)} %bitcast.79), calls=%async_computation.1 | async-start | bytes 262144 | tf_op jit(solution)/shard_map/all_to_all | solution.py:101
  46.4 9.5 %copy-start.4 = (bf16[1,32,2048]{2,1,0:T(8,128)(2,1)S(1)}, bf16[1,32,2048]{2,1,0:T(8,128)(2,1)}, u32[]{:S(2)}) copy-start(bf16[1,32,2048]{2,1,0:T(8,128)(2,1)} %param.10) | copy-start | bytes 393220
  57.2 25.8 %all-to-all-start.2 = ((bf16[64,8,128]{2,1,0:T(8,128)(2,1)}), bf16[64,8,128]{2,1,0:T(8,128)(2,1)S(1)}, u32[]{:S(2)}, u32[]{:S(2)}) async-start(bf16[64,8,128]{2,1,0:T(8,128)(2,1)} %bitcast.83), calls=%async_computation.2 | async-start | bytes 262144 | tf_op jit(solution)/shard_map/all_to_all | solution.py:102
  83.0 23.9 %all-to-all-start = ((bf16[64,1,32,128]{3,2,1,0:T(8,128)(2,1)}), bf16[64,1,32,128]{3,2,1,0:T(8,128)(2,1)S(1)}, u32[]{:S(2)}, u32[]{:S(2)}) async-start(bf16[64,1,32,128]{3,2,1,0:T(8,128)(2,1)} %constant_dynamic-update-slice_fusion), calls=%async_computation | async-start | bytes 1048576 | tf_op jit(solution)/shard_map/all_to_all | solution.py:91
  114.3 17.8 %all-to-all-start.4 = ((f32[64,1,32]{2,1,0:T(1,128)}), f32[64,1,32]{2,1,0:T(1,128)S(1)}, u32[]{:S(2)}, u32[]{:S(2)}) async-start(f32[64,1,32]{2,1,0:T(1,128)} %bitcast.87), calls=%async_computation.4 | async-start | bytes 65536 | tf_op jit(solution)/shard_map/all_to_all | solution.py:114
  148.0 4.9 %copy-start.3 = (bf16[1,32,2048]{2,1,0:T(8,128)(2,1)S(1)}, bf16[1,32,2048]{2,1,0:T(8,128)(2,1)}, u32[]{:S(2)}) copy-start(bf16[1,32,2048]{2,1,0:T(8,128)(2,1)} %param.9) | copy-start | bytes 393220
  148.0 37.3 %all-to-all-start.3 = ((f32[64,32,128]{2,1,0:T(8,128)}), f32[64,32,128]{2,1,0:T(8,128)S(1)}, u32[]{:S(2)}, u32[]{:S(2)}) async-start(f32[64,32,128]{2,1,0:T(8,128)} %bitcast.426), calls=%async_computation.3 | async-start | bytes 2097152 | tf_op jit(solution)/shard_map/all_to_all | solution.py:107
  152.9 29.0 %collective-permute-start.2 = (bf16[32,2048]{1,0:T(8,128)(2,1)S(1)}, bf16[32,2048]{1,0:T(8,128)(2,1)S(1)}, u32[]{:S(2)}, u32[]{:S(2)}) collective-permute-start(bf16[32,2048]{1,0:T(8,128)(2,1)S(1)} %bitcast.433), channel_id=1, source_target_pairs={{0,64},{64,128},{128,192},{192,256},{256,320},{320,384},{384,448},... | collective-permute-start | bytes 393224 | tf_op jit(solution)/shard_map/ppermute | solution.py:13
  156.0 25.9 %collective-permute-start.3 = (bf16[32,2048]{1,0:T(8,128)(2,1)S(1)}, bf16[32,2048]{1,0:T(8,128)(2,1)S(1)}, u32[]{:S(2)}, u32[]{:S(2)}) collective-permute-start(bf16[32,2048]{1,0:T(8,128)(2,1)S(1)} %bitcast.434), channel_id=1, source_target_pairs={{0,448},{64,0},{128,64},{192,128},{256,192},{320,256},{384,320},{4... | collective-permute-start | bytes 393224 | tf_op jit(solution)/shard_map/ppermute | solution.py:13
  160.3 24.4 %collective-permute-start = (bf16[32,2048]{1,0:T(8,128)(2,1)S(1)}, bf16[32,2048]{1,0:T(8,128)(2,1)S(1)}, u32[]{:S(2)}, u32[]{:S(2)}) collective-permute-start(bf16[32,2048]{1,0:T(8,128)(2,1)S(1)} %bitcast.436), channel_id=1, source_target_pairs={{0,64},{64,128},{128,192},{192,256},{256,320},{320,384},{384,448},... | collective-permute-start | bytes 393224 | tf_op jit(solution)/shard_map/ppermute | solution.py:13
  162.2 22.5 %collective-permute-start.1 = (bf16[32,2048]{1,0:T(8,128)(2,1)S(1)}, bf16[32,2048]{1,0:T(8,128)(2,1)S(1)}, u32[]{:S(2)}, u32[]{:S(2)}) collective-permute-start(bf16[32,2048]{1,0:T(8,128)(2,1)S(1)} %bitcast.437), channel_id=1, source_target_pairs={{0,448},{64,0},{128,64},{192,128},{256,192},{320,256},{384,320},{4... | collective-permute-start | bytes 393224 | tf_op jit(solution)/shard_map/ppermute | solution.py:13
  168.4 0.9 copy-start.2
